TPU v7x, 512 devices: a whole 4x8x8 slice. The times are simulated.
512 devices in a mesh: seq: 128 (over z, y, core), tp: 4 (over x).
Axes of the slice: x: 4, y: 8, z: 8, core: 2. Of those that a mesh axis runs over, the one named last changes fastest.
Arguments:
- queries: bfloat16 [32768, 4096], P('seq', 'tp'), may hold values from -6 to 6, as said below
- keys: bfloat16 [32768, 512], P('seq', 'tp'), may hold values from -6 to 6, as said below
- values: bfloat16 [32768, 512], P('seq', 'tp'), may hold values from -6 to 6
- segment: int32 [32768], P('seq'), may hold values from 0 to 255, never falling along the last dimension, each value on 1 to 512 neighbouring positions
- repack: int32 [32768], P('seq'), may hold values from 0 to 32767, as said below
- proj: bfloat16 [1536, 4096], P('seq', 'tp'), may hold values from -0.5 to 0.5
- student_states: bfloat16 [32768, 1536], P('seq'), may hold values from -6 to 6
- target_row: int32 [32768], P('seq'), may hold values from 0 to 255
Outputs:
- student_rows: bfloat16 [32768, 1536], P('seq', 'tp')
- grad: float32 [1536, 4096], P('seq', 'tp')
Inputs may be any that keep to these rules, and one draw needn't show every extreme that they name: `queries`: scaled normal entries. `keys`: scaled normal entries. `repack`: A permutation of the student rows. Each device's teacher rows go in consecutive groups of 4 rows, in order, each group to one student owner (the device holding student rows owner * 256 to owner * 256 + 255); every device sends exactly 4 rows to each of 64 other devices and none to itself, so at most 4 rows from one device to one owner, reached by every sending pair.
All inputs are finite; a program needn't handle non-finite values.
Results may differ from a plain program's by a relative error of at most 0.0056.
Values may be sent and summed in bfloat16 or wider, within the bound.
No kernel may reach another device: no remote copies, remote signals or barrier semaphores. Data moves between devices by JAX's collectives and lax.ppermute only.
A program may use at most 64 MiB of HBM per device.

v0:
```python
import math
import jax
import jax.numpy as jnp
from jax import lax
from jax.sharding import PartitionSpec as P

HEADS = 32
KV_HEADS = 4
HEAD_DIM = 128
SW = 1536
REACH = 2
neg_large = -1e30


def prefix(value, axis, combine, identity):
    size, here = (lax.axis_size(axis), lax.axis_index(axis))
    everything = jax.tree.map(lambda part: lax.all_gather(part, axis), value)
    start = jax.tree.map(
        lambda part, zero: jnp.broadcast_to(jnp.asarray(zero, part.dtype), part.shape),
        value,
        identity,
    )

    def hop(k, before):
        reached = k < here
        new = combine(before, jax.tree.map(lambda part: part[k], everything))
        return jax.tree.map(lambda a, b: jnp.where(reached, a, b), new, before)

    return lax.fori_loop(0, size, hop, start)


def passed_along(block, axis, distance):
    devices = range(lax.axis_size(axis))
    route = [(i - distance, i) for i in devices if i - distance in devices]
    return lax.ppermute(block, axis, route)


def anchor_combine(earlier, later):
    first_id = jnp.where(earlier[0] < 0, later[0], earlier[0])
    last_id = jnp.where(later[1] < 0, earlier[1], later[1])
    whole_later = (later[0] == later[1]) & (later[0] == earlier[1]) & (later[0] >= 0)
    start_pos = jnp.where(later[1] < 0, earlier[2], jnp.where(whole_later, earlier[2], later[2]))
    return (first_id, last_id, start_pos)


def document_starts(segment):
    row_count = segment.shape[0]
    row_pos = lax.axis_index("seq") * row_count + jnp.arange(row_count, dtype=jnp.int32)
    first_id = segment[0]
    last_id = segment[-1]
    last_start = jnp.min(jnp.where(segment == last_id, row_pos, jnp.int32(2**30)))
    sentinel = jnp.int32(-1)
    carried = prefix(
        (first_id, last_id, last_start), "seq", anchor_combine, (sentinel, sentinel, sentinel)
    )
    is_new = jnp.concatenate([jnp.ones((1,), bool), segment[1:] != segment[:-1]])
    local_start = lax.cummax(jnp.where(is_new, row_pos, jnp.int32(-1)), axis=0)
    inherit = (segment == carried[1]) & (segment == first_id)
    return (jnp.where(inherit, carried[2], local_start), row_pos)


def attend(queries, keys, values, row_start, row_pos):
    row_count = queries.shape[0]
    key_list = [keys]
    value_list = [values]
    pos_list = [row_pos]
    for step in range(1, REACH + 1):
        earlier = passed_along((keys, values), "seq", step)
        key_list.insert(0, earlier[0])
        value_list.insert(0, earlier[1])
        pos_list.insert(0, row_pos - step * row_count)
    all_keys = jnp.concatenate(key_list, axis=0)
    all_values = jnp.concatenate(value_list, axis=0)
    key_pos = jnp.concatenate(pos_list, axis=0)
    allowed = (key_pos[None, :] >= row_start[:, None]) & (key_pos[None, :] <= row_pos[:, None])
    kv_local = keys.shape[1] // HEAD_DIM
    group = HEADS // KV_HEADS
    part_size = 1
    q_heads = queries.reshape(row_count, kv_local, group, HEAD_DIM)
    scale = 1.0 / math.sqrt(HEAD_DIM)
    outputs = []
    for first in range(0, group, part_size):
        q_part = q_heads[:, 0, first : first + part_size, :]
        scores = (
            jnp.einsum("tjd,sd->jts", q_part, all_keys, preferred_element_type=jnp.float32) * scale
        )
        scores = jnp.where(allowed[None], scores, neg_large)
        top = jnp.max(scores, axis=-1, keepdims=True)
        expo = jnp.exp(scores - top)
        weights = (expo / jnp.sum(expo, axis=-1, keepdims=True)).astype(jnp.bfloat16)
        mixed = jnp.einsum("jts,sd->tjd", weights, all_values, preferred_element_type=jnp.float32)
        outputs.append(mixed.astype(jnp.bfloat16))
    return jnp.concatenate(outputs, axis=1).reshape(row_count, -1)


def project_rows(row_data, proj):
    return jnp.einsum(
        "tf,nf->tn",
        row_data,
        lax.all_gather(proj, "seq", axis=0, tiled=True),
        preferred_element_type=jnp.float32,
    )


def fill_buckets(data, target_dev, slot_rank, devices, capacity):
    empty = jnp.zeros((devices, capacity, data.shape[1]), data.dtype)
    return empty.at[target_dev, slot_rank].set(data)


def place_rows(received, slots, row_count):
    width = received.shape[-1]
    holder = jnp.zeros((row_count + 1, width), received.dtype)
    holder = holder.at[slots.reshape(-1)].set(received.reshape(-1, width))
    return holder[:row_count]


def on_device(queries, keys, values, segment, repack, proj, student_states, target_row):
    row_count = queries.shape[0]
    devices = lax.axis_size("seq")
    row_start, row_pos = document_starts(segment)
    attended = attend(queries, keys, values, row_start, row_pos)
    capacity = max(2 * row_count // devices, 2)
    target_dev = repack // row_count
    local_slot = repack - target_dev * row_count
    same_dev = target_dev[:, None] == target_dev[None, :]
    row_ids = jnp.arange(row_count, dtype=jnp.int32)
    before = row_ids[None, :] < row_ids[:, None]
    slot_rank = jnp.sum((same_dev & before).astype(jnp.int32), axis=1)
    slot_table = (
        jnp.full((devices, capacity), row_count, jnp.int32)
        .at[target_dev, slot_rank]
        .set(local_slot)
    )
    width_share = SW // lax.axis_size("tp")
    tp_index = lax.axis_index("tp")
    targets = student_states[target_row]
    buckets = fill_buckets(attended, target_dev, slot_rank, devices, capacity)
    arrived = (
        lax.all_to_all(buckets, "seq", split_axis=0, concat_axis=0, tiled=True),
        lax.all_to_all(slot_table, "seq", split_axis=0, concat_axis=0, tiled=True),
    )
    student_x = place_rows(arrived[0], arrived[1], row_count)
    y_part = project_rows(student_x, proj)
    y_total = lax.psum(y_part, "tp")
    y_rounded = y_total.astype(jnp.bfloat16)
    delta = (y_rounded.astype(jnp.float32) - targets.astype(jnp.float32)).astype(jnp.bfloat16)
    out_rows = lax.dynamic_slice_in_dim(y_rounded, tp_index * width_share, width_share, 1)
    norm_factor = 1.0 / math.sqrt(row_count * devices)
    grad_rows = delta.shape[1] // devices
    term = jnp.einsum("ts,tf->sf", delta, student_x, preferred_element_type=jnp.float32)
    pieces = term.reshape(devices, grad_rows, term.shape[1])
    summed = lax.all_to_all(
        pieces.astype(jnp.bfloat16), "seq", split_axis=0, concat_axis=0, tiled=True
    ).astype(pieces.dtype)
    grad = jnp.sum(summed, axis=0) * norm_factor
    return (out_rows, grad)


def solution(mesh):
    placed = (
        P("seq", "tp"),
        P("seq", "tp"),
        P("seq", "tp"),
        P("seq"),
        P("seq"),
        P("seq", "tp"),
        P("seq", None),
        P("seq"),
    )
    return jax.shard_map(
        on_device,
        mesh=mesh,
        in_specs=placed,
        out_specs=(P("seq", "tp"), P("seq", "tp")),
        check_vma=False,
    )
```

profile of v0, /device:TPU:41, one launch (start us, length us, event | category | flops | bytes accessed | tf_op | source)
XLA Modules:
  0.0 1131.9 jit_solution(2342865572813222749)
XLA Ops:
  7.2 2.4 collective-permute-start
  9.7 3.1 collective-permute-start.1
  12.8 3.2 collective-permute-start.2
  16.1 2.2 collective-permute-start.3
  18.3 0.7 multiply_subtract_fusion
  19.2 11.1 scatter_fusion
  30.3 0.7 copy.34
  31.0 15.8 %all-to-all-start = ((s32[128,1,4]{2,1,0:T(1,128)}), s32[128,1,4]{2,1,0:T(1,128)S(1)}, u32[]{:S(2)}, u32[]{:S(2)}) async-start(s32[128,1,4]{2,1,0:T(1,128)} %copy.34), calls=%async_computation | async-start | bytes 131072 | tf_op jit(solution)/shard_map/all_to_all | solution.py:140
  46.9 1.2 copy.35
  48.9 1.3 dynamic-slice
  50.1 1.2 fusion.59
  52.0 1.3 fusion.56
  53.3 1.3 dynamic-update-slice.2
  54.6 18.9 %all-reduce.3 = (s32[128]{0:T(128)S(1)}, s32[128]{0:T(128)S(1)}, s32[128]{0:T(128)S(1)}) all-reduce(s32[128]{0:T(128)S(1)} %get-tuple-element.149, s32[128]{0:T(128)S(1)} %slice_dynamic-update-slice_fusion, s32[128]{0:T(128)S(1)} %dynamic-update-slice.2), channel_id=1, replica_groups=mesh['seq'=128,'tp'=4] {'seq'}, use_global_device_ids=true, to_apply=%add | all-reduce | flops 384 | bytes 3072
  73.5 786.0 %while.15 = (s32[]{:T(128)}, s32[]{:T(128)}, s32[]{:T(128)}, s32[]{:T(128)}, s32[128]{0:T(128)S(1)}, /*index=5*/s32[128]{0:T(128)S(1)}, s32[128]{0:T(128)S(1)}, s32[]{:T(128)}, s32[]{:T(128)}) while((s32[]{:T(128)}, s32[]{:T(128)}, s32[]{:T(128)}, s32[]{:T(128)}, s32[128]{0:T(128)S(1)}, /*index=5*/s32[128]{0:T(128)S(1)}, s32[128]{0:T(128)S(1)}, ...), condition=%wide.region_4.5_spmd, body=%wide.region_3.4_spmd.sunk | while | flops 14 | bytes 261 | solution.py:29
  75.2 0.7 dynamic_slice.30
  81.4 0.7 dynamic_slice.30
  87.5 0.7 dynamic_slice.30
  99.8 0.7 dynamic_slice.30
  105.9 0.7 dynamic_slice.30
  112.1 0.7 dynamic_slice.30
  118.2 0.7 dynamic_slice.30
  124.3 0.7 dynamic_slice.30
  136.6 0.7 dynamic_slice.30
  142.8 0.7 dynamic_slice.30
  155.0 0.7 dynamic_slice.30
  161.2 0.7 dynamic_slice.30
  167.3 0.7 dynamic_slice.30
  173.5 0.7 dynamic_slice.30
  179.6 0.7 dynamic_slice.30
  185.8 0.7 dynamic_slice.30
  859.6 0.7 and_select_fusion
  866.9 1.2 broadcast_in_dim.35
  868.1 36.8 %scatter_fusion.1 = bf16[128,4,1024]{2,1,0:T(4,128)(2,1)} fusion(bf16[128,4,1024]{2,1,0:T(4,128)(2,1)} %broadcast_in_dim.35, s32[256]{0:T(256)S(1)} %bitcast.214, bf16[256,1024]{1,0:T(8,128)(2,1)S(1)} %copy.44), kind=kCustom, calls=%fused_computation.2 | custom fusion | bytes 1574912 | tf_op jit(solution)/shard_map/scatter | solution.py:107
  904.9 15.5 %all-to-all-start.1 = ((bf16[128,4,1024]{2,1,0:T(4,128)(2,1)}), bf16[128,4,1024]{2,1,0:T(4,128)(2,1)S(1)}, u32[]{:S(2)}, u32[]{:S(2)}) async-start(bf16[128,4,1024]{2,1,0:T(4,128)(2,1)} %scatter_fusion.1), calls=%async_computation.1 | async-start | bytes 2097152 | tf_op jit(solution)/shard_map/all_to_all | solution.py:139
  920.5 2.1 gather_fusion
  923.1 0.8 reduce.21
  924.1 25.2 %all-to-all-done.1 = bf16[128,4,1024]{2,1,0:T(4,128)(2,1)S(1)} async-done(((bf16[128,4,1024]{2,1,0:T(4,128)(2,1)}), bf16[128,4,1024]{2,1,0:T(4,128)(2,1)S(1)}, u32[]{:S(2)}, u32[]{:S(2)}) %all-to-all-start.1) | async-done | bytes 1048608 | tf_op jit(solution)/shard_map/all_to_all | solution.py:139
  949.5 2.8 scatter_custom_fusion.2
  952.3 6.2 reshape.408
  958.5 2.9 fusion.41
  961.4 34.9 %all-reduce.5 = bf16[256,1536]{1,0:T(8,128)(2,1)} all-reduce(f32[256,1536]{1,0:T(8,128)S(1)} %fusion.41), channel_id=1, replica_groups=mesh['seq'=128,'tp'=4] {'tp'}, use_global_device_ids=true, to_apply=%region_25.26 | all-reduce | flops 393216 | bytes 2359296 | tf_op jit(solution)/shard_map/psum | solution.py:144
  996.3 4.1 convolution_convert_fusion
  1000.4 6.1 convert_element_type.158
  1006.4 11.2 all-to-all-start.2
  1017.7 1.6 constant_dynamic-slice_fusion
  1019.3 102.1 %all-to-all-done.2 = bf16[128,12,1024]{2,1,0:T(8,128)(2,1)} async-done(((bf16[128,12,1024]{2,1,0:T(8,128)(2,1)}), bf16[128,12,1024]{2,1,0:T(8,128)(2,1)}, u32[]{:S(2)}, u32[]{:S(2)}) %all-to-all-start.2) | async-done | bytes 3145760 | tf_op jit(solution)/shard_map/all_to_all | solution.py:152
  1121.4 3.0 convert_reduce_fusion
  (441 shorter events, 231.6 us)
Async XLA Ops:
  7.2 913.3 %copy-start = (bf16[256,1536]{1,0:T(8,128)(2,1)S(1)}, bf16[256,1536]{1,0:T(8,128)(2,1)}, u32[]{:S(2)}) copy-start(bf16[256,1536]{1,0:T(8,128)(2,1)} %param.16) | copy-start | bytes 2359300
  7.2 853.1 %copy-start.1 = (bf16[256,128]{1,0:T(8,128)(2,1)S(1)}, bf16[256,128]{1,0:T(8,128)(2,1)}, u32[]{:S(2)}) copy-start(bf16[256,128]{1,0:T(8,128)(2,1)} %param.11) | copy-start | bytes 196612
  7.2 41.0 %copy-start.3 = (s32[256]{0:T(256)S(1)}, s32[256]{0:T(256)}, u32[]{:S(2)}) copy-start(s32[256]{0:T(256)} %param.13) | copy-start | bytes 3076
  7.2 945.1 %all-gather.3.cloned.1.call-start = ((), (), s32[]{:S(2)}) async-start(), calls=%async_computation.3 | async-start | bytes 4227072 | tf_op jit(solution)/shard_map/all_gather | solution.py:100
  7.2 854.4 %collective-permute-start = (bf16[256,128]{1,0:T(8,128)(2,1)}, bf16[256,128]{1,0:T(8,128)(2,1)S(1)}, u32[]{:S(2)}, u32[]{:S(2)}) collective-permute-start(bf16[256,128]{1,0:T(8,128)(2,1)} %param.12), channel_id=1, source_target_pairs={{0,8},{4,12},{8,16},{12,20},{16,24},{20,28},{24,32},{28,36},{32,40... | collective-permute-start | bytes 196616 | tf_op jit(solution)/shard_map/ppermute | solution.py:35
  9.7 852.0 %collective-permute-start.1 = (bf16[256,128]{1,0:T(8,128)(2,1)}, bf16[256,128]{1,0:T(8,128)(2,1)S(1)}, u32[]{:S(2)}, u32[]{:S(2)}) collective-permute-start(bf16[256,128]{1,0:T(8,128)(2,1)} %param.12), channel_id=1, source_target_pairs={{0,4},{4,8},{8,12},{12,16},{16,20},{20,24},{24,28},{28,32},{32,36}... | collective-permute-start | bytes 196616 | tf_op jit(solution)/shard_map/ppermute | solution.py:35
  12.8 847.4 %collective-permute-start.2 = (bf16[256,128]{1,0:T(8,128)(2,1)}, bf16[256,128]{1,0:T(8,128)(2,1)S(1)}, u32[]{:S(2)}, u32[]{:S(2)}) collective-permute-start(bf16[256,128]{1,0:T(8,128)(2,1)} %param.11), channel_id=1, source_target_pairs={{0,8},{4,12},{8,16},{12,20},{16,24},{20,28},{24,32},{28,36},{32,40... | collective-permute-start | bytes 196616 | tf_op jit(solution)/shard_map/ppermute | solution.py:35
  16.1 844.2 %collective-permute-start.3 = (bf16[256,128]{1,0:T(8,128)(2,1)}, bf16[256,128]{1,0:T(8,128)(2,1)S(1)}, u32[]{:S(2)}, u32[]{:S(2)}) collective-permute-start(bf16[256,128]{1,0:T(8,128)(2,1)} %param.11), channel_id=1, source_target_pairs={{0,4},{4,8},{8,12},{12,16},{16,20},{20,24},{24,28},{28,32},{32,36}... | collective-permute-start | bytes 196616 | tf_op jit(solution)/shard_map/ppermute | solution.py:35
  31.0 873.9 %all-to-all-start = ((s32[128,1,4]{2,1,0:T(1,128)}), s32[128,1,4]{2,1,0:T(1,128)S(1)}, u32[]{:S(2)}, u32[]{:S(2)}) async-start(s32[128,1,4]{2,1,0:T(1,128)} %copy.34), calls=%async_computation | async-start | bytes 131072 | tf_op jit(solution)/shard_map/all_to_all | solution.py:140
  860.3 1.4 copy-start.2
  868.1 52.3 %copy-start.4 = (s32[256]{0:T(256)S(1)}, s32[256]{0:T(256)}, u32[]{:S(2)}) copy-start(s32[256]{0:T(256)} %param.17) | copy-start | bytes 3076
  904.9 44.3 %all-to-all-start.1 = ((bf16[128,4,1024]{2,1,0:T(4,128)(2,1)}), bf16[128,4,1024]{2,1,0:T(4,128)(2,1)S(1)}, u32[]{:S(2)}, u32[]{:S(2)}) async-start(bf16[128,4,1024]{2,1,0:T(4,128)(2,1)} %scatter_fusion.1), calls=%async_computation.1 | async-start | bytes 2097152 | tf_op jit(solution)/shard_map/all_to_all | solution.py:139
  1006.4 114.9 %all-to-all-start.2 = ((bf16[128,12,1024]{2,1,0:T(8,128)(2,1)}), bf16[128,12,1024]{2,1,0:T(8,128)(2,1)}, u32[]{:S(2)}, u32[]{:S(2)}) async-start(bf16[128,12,1024]{2,1,0:T(8,128)(2,1)} %convert_element_type.158), calls=%async_computation.2 | async-start | bytes 8388608 | tf_op jit(solution)/shard_map/all_to_all | solution.py:152
Sparse Core Ops, SparseCore 0:
  18.4 86.5 all-gather.2
where the time goes:
time: 1140 us; the launch traced here: 1130 us
  loops' own time  554 us (49%)
  local copies, waits for them, and re-layouts  308 us (27%)
  waiting for transfers between devices  127 us (11%)
  blocking collectives  53.8 us (5%)
  starting transfers between devices  53.6 us (5%)
  between operations  14.4 us (1%)
  matrix products  11.8 us (1%)
    another operation x1, loops' own time, prefix(): return lax.fori_loop(0, size, hop, start)  554 us
    dynamic_slice x384, local copies, waits for them, and re-layouts, hop(): new = combine(before, jax.tree.map(lambda part: part[k], everything))  232 us
    all_to_all x1, waiting for transfers between devices, on_device(): lax.all_to_all(pieces.astype(jnp.bfloat16), 'seq', split_axis=0, concat_a...  102 us
    scatter x1, local copies, waits for them, and re-layouts, fill_buckets(): return empty.at[target_dev, slot_rank].set(data)  36.8 us
    psum x1, blocking collectives, on_device(): y_total = lax.psum(y_part, 'tp')  34.9 us
    all_to_all x1, waiting for transfers between devices, on_device(): lax.all_to_all(buckets, 'seq', split_axis=0, concat_axis=0, tiled=True)  25.2 us
  transfers between devices with their start and end apart: 8, of which 2 were waited for; matrix products, arithmetic and copies ran while one was open for 27% of the time, Pallas kernels for 0%

commit v1 on v0

--- a/solution.py
+++ b/solution.py
@@ -10,6 +10,14 @@
 SW = 1536
 REACH = 2
 neg_large = -1e30
+
+
+def sum_by_hops(block, name):
+    peers, result = (lax.axis_size(name), block)
+    for hop in [1 << k for k in range(peers.bit_length() - 1)]:
+        swap = [(i, i ^ hop) for i in range(peers)]
+        result = result + lax.ppermute(result, name, swap)
+    return result
 
 
 def prefix(value, axis, combine, identity):
@@ -141,7 +149,7 @@
     )
     student_x = place_rows(arrived[0], arrived[1], row_count)
     y_part = project_rows(student_x, proj)
-    y_total = lax.psum(y_part, "tp")
+    y_total = sum_by_hops(y_part, "tp")
     y_rounded = y_total.astype(jnp.bfloat16)
     delta = (y_rounded.astype(jnp.float32) - targets.astype(jnp.float32)).astype(jnp.bfloat16)
     out_rows = lax.dynamic_slice_in_dim(y_rounded, tp_index * width_share, width_share, 1)

time: 1140 us -> 1180 us (1.035)
  the two profiles are of different devices: /device:TPU:41 before, /device:TPU:33 now
where the time goes in v1:
time: 1180 us; the launch traced here: 1170 us
  loops' own time  554 us (47%)
  local copies, waits for them, and re-layouts  309 us (26%)
  waiting for transfers between devices  192 us (16%)
  starting transfers between devices  62.5 us (5%)
  blocking collectives  19 us (2%)
  between operations  14.5 us (1%)
    another operation x1, loops' own time, prefix(): return lax.fori_loop(0, size, hop, start)  554 us
    dynamic_slice x384, local copies, waits for them, and re-layouts, hop(): new = combine(before, jax.tree.map(lambda part: part[k], everything))  232 us
    all_to_all x1, waiting for transfers between devices, on_device(): lax.all_to_all(pieces.astype(jnp.bfloat16), 'seq', split_axis=0, concat_a...  101 us
    ppermute x2, waiting for transfers between devices, sum_by_hops(): result = result + lax.ppermute(result, name, swap)  65.3 us
    scatter x1, local copies, waits for them, and re-layouts, fill_buckets(): return empty.at[target_dev, slot_rank].set(data)  36.6 us
    all_to_all x1, waiting for transfers between devices, on_device(): lax.all_to_all(buckets, 'seq', split_axis=0, concat_axis=0, tiled=True)  26.4 us
  transfers between devices with their start and end apart: 10, of which 4 were waited for; matrix products, arithmetic and copies ran while one was open for 26% of the time, Pallas kernels for 0%

profile of v1, /device:TPU:33, one launch (start us, length us, event | category | flops | bytes accessed | tf_op | source)
XLA Modules:
  0.0 1172.5 jit_solution(17641855486841315615)
XLA Ops:
  7.2 2.4 collective-permute-start
  9.7 3.1 collective-permute-start.1
  12.8 2.3 collective-permute-start.2
  15.2 2.2 collective-permute-start.3
  17.4 0.7 multiply_subtract_fusion
  18.3 11.1 scatter_fusion
  29.4 0.7 copy.34
  30.1 16.8 %all-to-all-start = ((s32[128,1,4]{2,1,0:T(1,128)}), s32[128,1,4]{2,1,0:T(1,128)S(1)}, u32[]{:S(2)}, u32[]{:S(2)}) async-start(s32[128,1,4]{2,1,0:T(1,128)} %copy.34), calls=%async_computation | async-start | bytes 131072 | tf_op jit(solution)/shard_map/all_to_all | solution.py:148
  47.0 1.2 copy.35
  49.0 1.3 dynamic-slice
  50.2 1.2 fusion.59
  52.1 1.3 fusion.56
  53.4 1.3 dynamic-update-slice.2
  54.7 19.0 %all-reduce.3 = (s32[128]{0:T(128)S(1)}, s32[128]{0:T(128)S(1)}, s32[128]{0:T(128)S(1)}) all-reduce(s32[128]{0:T(128)S(1)} %get-tuple-element.149, s32[128]{0:T(128)S(1)} %slice_dynamic-update-slice_fusion, s32[128]{0:T(128)S(1)} %dynamic-update-slice.2), channel_id=1, replica_groups=mesh['seq'=128,'tp'=4] {'seq'}, use_global_device_ids=true, to_apply=%add | all-reduce | flops 384 | bytes 3072
  73.7 786.0 %while.15 = (s32[]{:T(128)}, s32[]{:T(128)}, s32[]{:T(128)}, s32[]{:T(128)}, s32[128]{0:T(128)S(1)}, /*index=5*/s32[128]{0:T(128)S(1)}, s32[128]{0:T(128)S(1)}, s32[]{:T(128)}, s32[]{:T(128)}) while((s32[]{:T(128)}, s32[]{:T(128)}, s32[]{:T(128)}, s32[]{:T(128)}, s32[128]{0:T(128)S(1)}, /*index=5*/s32[128]{0:T(128)S(1)}, s32[128]{0:T(128)S(1)}, ...), condition=%wide.region_4.5_spmd, body=%wide.region_3.4_spmd.sunk | while | flops 14 | bytes 261 | solution.py:37
  81.5 0.7 dynamic_slice.30
  87.7 0.7 dynamic_slice.30
  93.8 0.7 dynamic_slice.30
  100.0 0.7 dynamic_slice.30
  106.1 0.7 dynamic_slice.30
  112.2 0.7 dynamic_slice.30
  118.4 0.7 dynamic_slice.30
  130.7 0.7 dynamic_slice.30
  136.8 0.7 dynamic_slice.30
  142.9 0.7 dynamic_slice.30
  149.1 0.7 dynamic_slice.30
  859.7 0.7 and_select_fusion
  867.1 1.2 broadcast_in_dim.35
  868.4 36.6 %scatter_fusion.1 = bf16[128,4,1024]{2,1,0:T(4,128)(2,1)} fusion(bf16[128,4,1024]{2,1,0:T(4,128)(2,1)} %broadcast_in_dim.35, s32[256]{0:T(256)S(1)} %bitcast.214, bf16[256,1024]{1,0:T(8,128)(2,1)S(1)} %copy.44), kind=kCustom, calls=%fused_computation.2 | custom fusion | bytes 1574912 | tf_op jit(solution)/shard_map/scatter | solution.py:115
  904.9 15.6 %all-to-all-start.1 = ((bf16[128,4,1024]{2,1,0:T(4,128)(2,1)}), bf16[128,4,1024]{2,1,0:T(4,128)(2,1)S(1)}, u32[]{:S(2)}, u32[]{:S(2)}) async-start(bf16[128,4,1024]{2,1,0:T(4,128)(2,1)} %scatter_fusion.1), calls=%async_computation.1 | async-start | bytes 2097152 | tf_op jit(solution)/shard_map/all_to_all | solution.py:147
  921.1 0.8 reduce.21
  922.0 26.4 %all-to-all-done.1 = bf16[128,4,1024]{2,1,0:T(4,128)(2,1)S(1)} async-done(((bf16[128,4,1024]{2,1,0:T(4,128)(2,1)}), bf16[128,4,1024]{2,1,0:T(4,128)(2,1)S(1)}, u32[]{:S(2)}, u32[]{:S(2)}) %all-to-all-start.1) | async-done | bytes 1048608 | tf_op jit(solution)/shard_map/all_to_all | solution.py:147
  948.7 2.8 scatter_custom_fusion.2
  951.5 6.2 reshape.408
  957.7 2.9 fusion.41
  960.6 3.1 collective-permute-start.4
  963.7 34.2 %collective-permute-done.4 = f32[256,1536]{1,0:T(8,128)S(1)} collective-permute-done((f32[256,1536]{1,0:T(8,128)S(1)}, f32[256,1536]{1,0:T(8,128)S(1)}, u32[]{:S(2)}, u32[]{:S(2)}) %collective-permute-start.4) | collective-permute-done | bytes 1572896 | tf_op jit(solution)/shard_map/ppermute | solution.py:19
  998.1 4.6 collective-permute-start.5
  1002.8 2.2 gather_fusion
  1005.0 31.2 %collective-permute-done.5 = f32[256,1536]{1,0:T(8,128)} collective-permute-done((f32[256,1536]{1,0:T(8,128)S(1)}, f32[256,1536]{1,0:T(8,128)}, u32[]{:S(2)}, u32[]{:S(2)}) %collective-permute-start.5) | collective-permute-done | bytes 1572896 | tf_op jit(solution)/shard_map/ppermute | solution.py:19
  1036.2 1.7 add_convert_fusion
  1037.9 0.9 copy-done.1
  1038.8 2.7 convolution_convert_fusion
  1041.5 6.1 convert_element_type.158
  1047.6 12.2 %all-to-all-start.2 = ((bf16[128,12,1024]{2,1,0:T(8,128)(2,1)}), bf16[128,12,1024]{2,1,0:T(8,128)(2,1)}, u32[]{:S(2)}, u32[]{:S(2)}) async-start(bf16[128,12,1024]{2,1,0:T(8,128)(2,1)} %convert_element_type.158), calls=%async_computation.2 | async-start | bytes 8388608 | tf_op jit(solution)/shard_map/all_to_all | solution.py:160
  1059.8 1.6 constant_dynamic-slice_fusion
  1061.4 100.6 %all-to-all-done.2 = bf16[128,12,1024]{2,1,0:T(8,128)(2,1)} async-done(((bf16[128,12,1024]{2,1,0:T(8,128)(2,1)}), bf16[128,12,1024]{2,1,0:T(8,128)(2,1)}, u32[]{:S(2)}, u32[]{:S(2)}) %all-to-all-start.2) | async-done | bytes 3145760 | tf_op jit(solution)/shard_map/all_to_all | solution.py:160
  1162.0 3.0 convert_reduce_fusion
  (450 shorter events, 235.1 us)
Async XLA Ops:
  7.2 995.7 %copy-start = (bf16[256,1536]{1,0:T(8,128)(2,1)S(1)}, bf16[256,1536]{1,0:T(8,128)(2,1)}, u32[]{:S(2)}) copy-start(bf16[256,1536]{1,0:T(8,128)(2,1)} %param.16) | copy-start | bytes 2359300
  7.2 853.3 %copy-start.3 = (bf16[256,128]{1,0:T(8,128)(2,1)S(1)}, bf16[256,128]{1,0:T(8,128)(2,1)}, u32[]{:S(2)}) copy-start(bf16[256,128]{1,0:T(8,128)(2,1)} %param.11) | copy-start | bytes 196612
  7.2 41.1 %copy-start.5 = (s32[256]{0:T(256)S(1)}, s32[256]{0:T(256)}, u32[]{:S(2)}) copy-start(s32[256]{0:T(256)} %param.13) | copy-start | bytes 3076
  7.2 944.3 %all-gather.3.cloned.1.call-start = ((), (), s32[]{:S(2)}) async-start(), calls=%async_computation.3 | async-start | bytes 4227072 | tf_op jit(solution)/shard_map/all_gather | solution.py:108
  7.2 854.6 %collective-permute-start = (bf16[256,128]{1,0:T(8,128)(2,1)}, bf16[256,128]{1,0:T(8,128)(2,1)S(1)}, u32[]{:S(2)}, u32[]{:S(2)}) collective-permute-start(bf16[256,128]{1,0:T(8,128)(2,1)} %param.12), channel_id=1, source_target_pairs={{0,8},{4,12},{8,16},{12,20},{16,24},{20,28},{24,32},{28,36},{32,40... | collective-permute-start | bytes 196616 | tf_op jit(solution)/shard_map/ppermute | solution.py:43
  9.7 852.2 %collective-permute-start.1 = (bf16[256,128]{1,0:T(8,128)(2,1)}, bf16[256,128]{1,0:T(8,128)(2,1)S(1)}, u32[]{:S(2)}, u32[]{:S(2)}) collective-permute-start(bf16[256,128]{1,0:T(8,128)(2,1)} %param.12), channel_id=1, source_target_pairs={{0,4},{4,8},{8,12},{12,16},{16,20},{20,24},{24,28},{28,32},{32,36}... | collective-permute-start | bytes 196616 | tf_op jit(solution)/shard_map/ppermute | solution.py:43
  12.8 847.6 %collective-permute-start.2 = (bf16[256,128]{1,0:T(8,128)(2,1)}, bf16[256,128]{1,0:T(8,128)(2,1)S(1)}, u32[]{:S(2)}, u32[]{:S(2)}) collective-permute-start(bf16[256,128]{1,0:T(8,128)(2,1)} %param.11), channel_id=1, source_target_pairs={{0,8},{4,12},{8,16},{12,20},{16,24},{20,28},{24,32},{28,36},{32,40... | collective-permute-start | bytes 196616 | tf_op jit(solution)/shard_map/ppermute | solution.py:43
  15.2 845.3 %collective-permute-start.3 = (bf16[256,128]{1,0:T(8,128)(2,1)}, bf16[256,128]{1,0:T(8,128)(2,1)S(1)}, u32[]{:S(2)}, u32[]{:S(2)}) collective-permute-start(bf16[256,128]{1,0:T(8,128)(2,1)} %param.11), channel_id=1, source_target_pairs={{0,4},{4,8},{8,12},{12,16},{16,20},{20,24},{24,28},{28,32},{32,36}... | collective-permute-start | bytes 196616 | tf_op jit(solution)/shard_map/ppermute | solution.py:43
  30.1 874.8 %all-to-all-start = ((s32[128,1,4]{2,1,0:T(1,128)}), s32[128,1,4]{2,1,0:T(1,128)S(1)}, u32[]{:S(2)}, u32[]{:S(2)}) async-start(s32[128,1,4]{2,1,0:T(1,128)} %copy.34), calls=%async_computation | async-start | bytes 131072 | tf_op jit(solution)/shard_map/all_to_all | solution.py:148
  860.5 1.4 copy-start.4
  904.9 43.5 %all-to-all-start.1 = ((bf16[128,4,1024]{2,1,0:T(4,128)(2,1)}), bf16[128,4,1024]{2,1,0:T(4,128)(2,1)S(1)}, u32[]{:S(2)}, u32[]{:S(2)}) async-start(bf16[128,4,1024]{2,1,0:T(4,128)(2,1)} %scatter_fusion.1), calls=%async_computation.1 | async-start | bytes 2097152 | tf_op jit(solution)/shard_map/all_to_all | solution.py:147
  960.6 42.2 %copy-start.6 = (s32[256]{0:T(256)S(1)}, s32[256]{0:T(256)}, u32[]{:S(2)}) copy-start(s32[256]{0:T(256)} %param.17) | copy-start | bytes 3076
  960.6 37.3 %collective-permute-start.4 = (f32[256,1536]{1,0:T(8,128)S(1)}, f32[256,1536]{1,0:T(8,128)S(1)}, u32[]{:S(2)}, u32[]{:S(2)}) collective-permute-start(f32[256,1536]{1,0:T(8,128)S(1)} %fusion.41), channel_id=1, source_target_pairs={{0,1},{1,0},{2,3},{3,2},{4,5},{5,4},{6,7},{7,6},{8,9},{9,8},{10,11... | collective-permute-start | bytes 4718600 | tf_op jit(solution)/shard_map/ppermute | solution.py:19
  998.1 38.0 %collective-permute-start.5 = (f32[256,1536]{1,0:T(8,128)S(1)}, f32[256,1536]{1,0:T(8,128)}, u32[]{:S(2)}, u32[]{:S(2)}) collective-permute-start(f32[256,1536]{1,0:T(8,128)S(1)} %add.90), channel_id=1, source_target_pairs={{0,2},{1,3},{2,0},{3,1},{4,6},{5,7},{6,4},{7,5},{8,10},{9,11},{10,... | collective-permute-start | bytes 4718600 | tf_op jit(solution)/shard_map/ppermute | solution.py:19
  1005.0 33.8 %copy-start.2 = (bf16[256,1536]{1,0:T(8,128)(2,1)S(1)}, bf16[256,1536]{1,0:T(8,128)(2,1)}, u32[]{:S(2)}) copy-start(bf16[256,1536]{1,0:T(8,128)(2,1)} %gather_fusion) | copy-start | bytes 2359300
  1037.9 0.9 copy-start.1
  1047.6 114.4 %all-to-all-start.2 = ((bf16[128,12,1024]{2,1,0:T(8,128)(2,1)}), bf16[128,12,1024]{2,1,0:T(8,128)(2,1)}, u32[]{:S(2)}, u32[]{:S(2)}) async-start(bf16[128,12,1024]{2,1,0:T(8,128)(2,1)} %convert_element_type.158), calls=%async_computation.2 | async-start | bytes 8388608 | tf_op jit(solution)/shard_map/all_to_all | solution.py:160
Sparse Core Ops, SparseCore 0:
  17.5 87.7 all-gather.2
